TPU v7x, 32 devices: a whole 2x2x4 slice. The times are simulated.
32 devices in a mesh: row: 8 (over z, core), col: 4 (over y, x).
Axes of the slice: x: 2, y: 2, z: 4, core: 2. Of those that a mesh axis runs over, the one named last changes fastest.
Arguments:
- context: bfloat16 [128, 16384], P('row', 'col'), may hold values from -6 to 6
- out_weight: bfloat16 [16384, 16384], P('col', 'row'), may hold values from -0.046875 to 0.046875
- residual: bfloat16 [128, 16384], P('col', 'row'), may hold values from -80 to 80
- teacher_gain: float32 [16384], replicated, may hold values from 0.5 to 1.5
- student_hidden: bfloat16 [128, 4096], P(('row', 'col')), may hold values from -6 to 6
- student_gain: float32 [4096], replicated, may hold values from 0.5 to 1.5
- projector: bfloat16 [4096, 16384], P(None, ('row', 'col')), may hold values from -0.09375 to 0.09375
Outputs:
- grad_proj: float32 [4096, 16384], P(None, ('row', 'col'))
- grad_gain: float32 [4096], replicated
- loss: float32 [], replicated
All inputs are finite; a program needn't handle non-finite values.
Results may differ from a plain program's by a relative error of at most 0.0065.
Values may be sent and summed in bfloat16 or wider, within the bound.
A program may use at most 64 MiB of HBM per device.

v0:
```python
import jax
import jax.numpy as jnp
from jax import lax
from jax.sharding import PartitionSpec as P

D_T = 16384


norm_eps = 1e-05


def normalize(hidden):
    widened = hidden.astype(jnp.float32)
    return widened * lax.rsqrt(jnp.mean(widened * widened, axis=1, keepdims=True) + norm_eps)


def per_device(
    context, out_weight, residual, teacher_gain, student_hidden, student_gain, projector
):
    row_index = lax.axis_index("row")
    context_all = lax.all_gather(context, "row", axis=0, tiled=True)
    out_block = out_weight.shape[1]
    summed = lax.psum_scatter(
        jnp.dot(context_all, out_weight, preferred_element_type=jnp.float32),
        "col",
        scatter_dimension=0,
        tiled=True,
    )
    summed = summed + residual.astype(jnp.float32)
    squares = lax.psum(jnp.sum(summed * summed, axis=1), "row")
    gain_block = lax.dynamic_slice_in_dim(teacher_gain, row_index * out_block, out_block)
    final_rows = (summed * lax.rsqrt(squares / D_T + norm_eps)[:, None] * gain_block).astype(
        jnp.bfloat16
    )
    target = lax.all_to_all(final_rows, "col", split_axis=1, concat_axis=0, tiled=True)
    hidden_all = lax.all_gather(student_hidden, ("row", "col"), axis=0, tiled=True)
    normed_all = normalize(hidden_all)
    student_all = (normed_all * student_gain).astype(jnp.bfloat16)
    predicted = jnp.dot(student_all, projector, preferred_element_type=jnp.float32)
    difference = predicted - target.astype(jnp.float32)
    loss_part = jnp.sum(difference * difference)
    loss_total = lax.psum(loss_part, ("row", "col"))
    error_term = (difference * (1.0 / 64.0)).astype(jnp.bfloat16)
    grad_proj = lax.dot_general(
        student_all, error_term, (((0,), (0,)), ((), ())), preferred_element_type=jnp.float32
    )
    grad_normed = lax.dot_general(
        error_term, projector, (((1,), (1,)), ((), ())), preferred_element_type=jnp.float32
    )
    gain_part = jnp.sum(grad_normed * normed_all, axis=0)
    grad_gain = lax.psum(gain_part, ("row", "col"))
    tokens_all = predicted.shape[0]
    loss = loss_total / (tokens_all * D_T)
    return (grad_proj, grad_gain, loss)


def solution(mesh):
    placed = (
        P("row", "col"),
        P("col", "row"),
        P("col", "row"),
        P(),
        P(("row", "col"), None),
        P(),
        P(None, ("row", "col")),
    )
    return jax.shard_map(
        per_device,
        mesh=mesh,
        in_specs=placed,
        out_specs=(P(None, ("row", "col")), P(), P()),
        check_vma=False,
    )
```

profile of v0, /device:TPU:0, one launch (start us, length us, event | category | flops | bytes accessed | tf_op | source)
XLA Modules:
  0.0 204.2 jit_solution(2190091404144003150)
XLA Ops:
  7.2 0.0 all-gather.4.cloned.1.call-start
  7.2 0.7 all-gather.4.cloned.1.call-update
  7.9 0.0 all-gather.6.cloned.1.call-start
  7.9 0.7 all-gather.6.cloned.1.call-update
  8.6 0.0 reduce-scatter.2.cloned.1.call-start
  8.7 25.9 %all-gather.4.cloned.1.call-done = bf16[128,4096]{1,0:T(8,128)(2,1)} async-done(((bf16[16,4096]{1,0:T(8,128)(2,1)}), bf16[128,4096]{1,0:T(8,128)(2,1)}) %all-gather.4.cloned.1.call-update) | async-done | bytes 1048592 | tf_op jit(solution)/shard_map/all_gather | solution.py:21
  34.6 9.4 %fusion.4 = f32[128,2048]{1,0:T(8,128)} fusion(bf16[128,4096]{1,0:T(8,128)(2,1)} %all-gather.4.cloned.1.call-done, bf16[4096,2048]{1,0:T(8,128)(2,1)} %param.8), kind=kOutput, calls=%fused_computation.16 | convolution fusion | flops 2147483648 | bytes 18874368 | tf_op jit(solution)/shard_map/dot_general | solution.py:24
  44.0 0.0 reduce-scatter.2.cloned.1.call-update
  44.0 0.0 copy-start.1
  44.0 0.0 dynamic-slice-start
  44.0 46.8 %all-gather.6.cloned.1.call-done = bf16[32,4,4096]{2,1,0:T(4,128)(2,1)} async-done(((bf16[1,4,4096]{2,1,0:T(4,128)(2,1)}), bf16[32,4,4096]{2,1,0:T(4,128)(2,1)}) %all-gather.6.cloned.1.call-update) | async-done | bytes 1048592 | tf_op jit(solution)/shard_map/all_gather | solution.py:36
  90.9 1.3 reshape.25
  92.2 0.0 copy-start.2
  92.2 0.2 multiply_reduce_fusion
  92.4 28.9 %reduce-scatter.2.cloned.1.call-done = f32[32,2048]{1,0:T(8,128)} async-done(((f32[128,2048]{1,0:T(8,128)}), f32[32,2048]{1,0:T(8,128)}) %reduce-scatter.2.cloned.1.call-update) | async-done | bytes 262160 | tf_op jit(solution)/shard_map/reduce_scatter | solution.py:23
  121.3 0.0 copy-done.1
  121.3 1.1 multiply_reduce_fusion.2
  122.4 16.2 %psum.21 = f32[32]{0:T(128)S(1)} all-reduce(f32[32]{0:T(128)S(1)} %multiply_reduce_fusion.2), channel_id=1, replica_groups=mesh['row'=8,'col'=4] {'row'}, use_global_device_ids=true, to_apply=%region_3.0 | all-reduce | flops 32 | bytes 256 | tf_op jit(solution)/shard_map/psum | solution.py:30
  138.6 0.0 dynamic-slice-done
  138.6 1.0 multiply_convert_fusion.2
  139.6 0.7 copy.14
  140.3 3.3 %all-to-all-start = ((bf16[32,4,512]{2,0,1:T(8,128)(2,1)}), bf16[32,4,512]{2,0,1:T(8,128)(2,1)S(1)}, u32[]{:S(2)}, u32[]{:S(2)}) async-start(bf16[32,4,512]{2,0,1:T(8,128)(2,1)} %bitcast.11), calls=%async_computation.1 | async-start | bytes 262144 | tf_op jit(solution)/shard_map/all_to_all | solution.py:35
  143.7 5.0 %all-to-all-done = bf16[32,4,512]{2,0,1:T(8,128)(2,1)S(1)} async-done(((bf16[32,4,512]{2,0,1:T(8,128)(2,1)}), bf16[32,4,512]{2,0,1:T(8,128)(2,1)S(1)}, u32[]{:S(2)}, u32[]{:S(2)}) %all-to-all-start) | async-done | bytes 131104 | tf_op jit(solution)/shard_map/all_to_all | solution.py:35
  148.7 0.0 copy-done.2
  148.7 0.0 copy-start
  148.7 3.7 %multiply_reduce_fusion.1 = (f32[]{:T(128)}, f32[128,512]{1,0:T(8,128)S(1)}) fusion(f32[128,512]{1,0:T(8,128)S(1)} %bitcast.12, bf16[4096,512]{1,0:T(8,128)(2,1)} %param.13, f32[128,4096]{1,0:T(8,128)S(1)} %reshape.25, f32[4096]{0:T(1024)S(1)} %copy-done.2, f32[128]{0:T(128)S(1)} %add_rsqrt_fusion.1), kind=kOutput, calls=%fused_computation.5 | convolution fusion | flops 538640384 | bytes 6832644 | tf_op jit(solution)/shard_map/dot_general | solution.py:39
  152.4 0.0 copy-done
  152.4 1.5 fusion
  153.9 4.8 %fusion.1 = f32[4096,512]{1,0:T(8,128)} fusion(f32[128,512]{1,0:T(8,128)S(1)} %get-tuple-element.6, f32[128,4096]{1,0:T(8,128)S(1)} %reshape.25, f32[4096]{0:T(1024)S(1)} %copy-done.2, f32[128]{0:T(128)S(1)} %add_rsqrt_fusion.1), kind=kOutput, calls=%fused_computation.11 | convolution fusion | flops 538574848 | bytes 10764800 | tf_op jit(solution)/shard_map/dot_general | solution.py:44
  158.7 37.2 %all-reduce = (f32[4096]{0:T(1024)}, f32[]{:T(128)}) all-reduce(f32[4096]{0:T(1024)S(1)} %fusion, f32[]{:T(128)} %get-tuple-element.5), channel_id=1, replica_groups=mesh['row'=8,'col'=4] {'row','col'}, use_global_device_ids=true, to_apply=%region_5.0 | all-reduce | flops 4097 | bytes 32776 | tf_op jit(solution)/shard_map/psum | solution.py:51
  (3 shorter events, 0.0 us)
Async XLA Ops:
  7.2 27.4 %all-gather.4.cloned.1.call-start = ((), (), s32[]{:S(2)}) async-start(), calls=%async_computation.2 | async-start | bytes 1179648 | tf_op jit(solution)/shard_map/all_gather | solution.py:21
  7.9 83.0 %all-gather.6.cloned.1.call-start = ((), (), s32[]{:S(2)}) async-start(), calls=%async_computation.4 | async-start | bytes 1081344 | tf_op jit(solution)/shard_map/all_gather | solution.py:36
  8.6 112.7 %reduce-scatter.2.cloned.1.call-start = ((), (), s32[]{:S(2)}) async-start(), calls=%async_computation.3 | async-start | bytes 1310720 | tf_op jit(solution)/shard_map/reduce_scatter | solution.py:23
  44.0 77.3 %copy-start.1 = (bf16[32,2048]{1,0:T(8,128)(2,1)S(1)}, bf16[32,2048]{1,0:T(8,128)(2,1)}, u32[]{:S(2)}) copy-start(bf16[32,2048]{1,0:T(8,128)(2,1)} %param.9) | copy-start | bytes 393220
  44.0 94.6 %dynamic-slice-start = ((f32[16384]{0:T(1024)}, s32[]{:T(128)}), f32[2048]{0:T(1024)S(1)}, s32[]{:S(2)}) async-start(f32[16384]{0:T(1024)} %param.10, s32[]{:T(128)} %select_n.3), calls=%async_computation.5 | async-start | bytes 16896 | tf_op jit(solution)/shard_map/dynamic_slice | solution.py:31
  92.2 56.5 %copy-start.2 = (f32[4096]{0:T(1024)S(1)}, f32[4096]{0:T(1024)}, u32[]{:S(2)}) copy-start(f32[4096]{0:T(1024)} %param.12) | copy-start | bytes 49156
  140.3 8.3 %all-to-all-start = ((bf16[32,4,512]{2,0,1:T(8,128)(2,1)}), bf16[32,4,512]{2,0,1:T(8,128)(2,1)S(1)}, u32[]{:S(2)}, u32[]{:S(2)}) async-start(bf16[32,4,512]{2,0,1:T(8,128)(2,1)} %bitcast.11), calls=%async_computation.1 | async-start | bytes 262144 | tf_op jit(solution)/shard_map/all_to_all | solution.py:35
  148.7 3.8 %copy-start = (bf16[4096,512]{1,0:T(8,128)(2,1)S(1)}, bf16[4096,512]{1,0:T(8,128)(2,1)}, u32[]{:S(2)}) copy-start(bf16[4096,512]{1,0:T(8,128)(2,1)} %param.13) | copy-start | bytes 12582916
Sparse Core Ops, SparseCore 0:
  9.6 24.9 all-gather.3
  37.6 53.2 all-gather.5
  94.3 26.9 reduce-scatter.1
where the time goes:
time: 206 us; the launch traced here: 204 us
  waiting for transfers between devices  108 us (52%)
  blocking collectives  53.4 us (26%)
  matrix products  19.4 us (9%)
  between operations  15.6 us (8%)
  starting transfers between devices  3.44 us (2%)
  other arithmetic  2.4 us (1%)
    all_gather x1, waiting for transfers between devices, per_device(): lax.all_gather(student_hidden, ('row', 'col'), axis=0, tiled=True)  46.8 us
    psum x1, blocking collectives, per_device(): grad_gain = lax.psum(gain_part, ('row', 'col'))  37.2 us
    reduce_scatter x1, waiting for transfers between devices, per_device(): lax.psum_scatter(jnp.dot(context_all, out_weight, preferred_element_type=...  28.9 us
    all_gather x1, waiting for transfers between devices, per_device(): context_all = lax.all_gather(context, 'row', axis=0, tiled=True)  25.9 us
    psum x1, blocking collectives, per_device(): squares = lax.psum(jnp.sum(summed * summed, axis=1), 'row')  16.2 us
    dot_general x1, matrix products, per_device(): jnp.dot(context_all, out_weight, preferred_element_type=jnp.float32)  9.41 us
    all_to_all x1, waiting for transfers between devices, per_device(): lax.all_to_all(final_rows, 'col', split_axis=1, concat_axis=0, tiled=True)  4.97 us
    dot_general x1, matrix products, per_device(): lax.dot_general(student_all, error_term, (((0,), (0,)), ((), ())), prefer...  4.76 us
  transfers between devices with their start and end apart: 4, of which 4 were waited for; matrix products, arithmetic and copies ran while one was open for 5% of the time, Pallas kernels for 0%

commit v1 on v0

v1 whole, which is shorter than its diff:
```python
import functools

import jax
import jax.numpy as jnp
from jax import lax
from jax.experimental import pallas as pl
from jax.experimental.pallas import tpu as pltpu
from jax.sharding import PartitionSpec as P

norm_eps = 1e-05
LANES = 128
CHUNKS = 4
MESH = pl.DeviceIdType.MESH


def to_row(column):
    return jnp.transpose(jnp.broadcast_to(column, (LANES, LANES)))[0:1, :]


def to_column(row):
    return jnp.transpose(jnp.broadcast_to(row, (LANES, LANES)))[:, 0:1]


def body(
    n_row, n_col,
    context, weight, residual, teacher_gain, hidden, student_gain, projector,
    student_out, error_out, gain_out, loss_out,
    ctx, w, proj, acc, part_out, part_in, res, hid, wide, inverse, sgain, tgain,
    predicted, total, sq_out, sq_in, gp, gp_in, gg_out, gg,
    local_sem, w_sem, ctx_send, ctx_recv, hid_chain, hid_partner, hid_col, hid_recv,
    col_send, col_recv, all_send, all_recv,
):
    devices = n_row * n_col
    chips = n_row // 2
    r, c = lax.axis_index("row"), lax.axis_index("col")
    me = r * n_col + c
    p, core = r // 2, r % 2
    tok = context.shape[0]
    features = context.shape[1]
    chunk = features // CHUNKS
    tokens = tok * n_row
    width = proj.shape[1]
    res_rows = residual.shape[0]
    hid_rows = hidden.shape[0]
    d_s = hidden.shape[1]
    d_t = width * devices
    segments = gain_out.shape[0]
    repeat = devices // segments

    def rows_of(row):
        return pl.ds(pl.multiple_of(row * tok, tok), tok)

    def row_of(pos):
        return pos * 2 + core

    own = [
        pltpu.make_async_copy(context, ctx.at[rows_of(r), :], local_sem.at[0]),
        pltpu.make_async_copy(hidden, hid.at[me], local_sem.at[1]),
        pltpu.make_async_copy(
            residual.at[:, pl.ds(pl.multiple_of(c * width, width), width)],
            res.at[pl.ds(pl.multiple_of(c * res_rows, res_rows), res_rows), :],
            local_sem.at[2],
        ),
    ]
    for copy in own:
        copy.start()

    def w_copy(k):
        part = pl.ds(k * chunk, chunk)
        return pltpu.make_async_copy(weight.at[part, :], w.at[part, :], w_sem.at[k])

    for k in range(CHUNKS):
        w_copy(k).start()
    proj_copy = pltpu.make_async_copy(projector, proj, local_sem.at[3])
    proj_copy.start()

    barrier = pltpu.get_barrier_semaphore()

    def greet(i, _):
        d = (me + 1 + i) % devices
        pl.semaphore_signal(
            barrier, inc=1, device_id=(d // n_col, d % n_col), device_id_type=MESH
        )
        return 0

    lax.fori_loop(0, devices - 1, greet, 0)
    pl.semaphore_wait(barrier, devices - 1)

    up, down, partner = (r + 2, c), (r - 2, c), (r + 1 - 2 * core, c)
    targets = {0: up, 1: down, 2: partner}

    def ctx_copy(pos, k, way, first=False):
        row = row_of(pos)
        cols = pl.ds(k * chunk, chunk)
        there = ctx.at[rows_of(row), cols]
        return pltpu.make_async_remote_copy(
            src_ref=context.at[:, cols] if first else there,
            dst_ref=there,
            send_sem=ctx_send.at[way, pos, k],
            recv_sem=ctx_recv.at[row, k],
            device_id=targets[way],
            device_id_type=MESH,
        )

    def hid_copy(row, col, device, send_sem, first=False):
        slot = row * n_col + col
        return pltpu.make_async_remote_copy(
            src_ref=hidden if first else hid.at[slot],
            dst_ref=hid.at[slot],
            send_sem=send_sem,
            recv_sem=hid_recv.at[slot],
            device_id=device,
            device_id_type=MESH,
        )

    def hid_way(pos, way, first=False):
        return hid_copy(row_of(pos), c, targets[way], hid_chain.at[way, pos], first)

    def hid_side(pos, i, first=False):
        return hid_copy(row_of(pos), c, (r, (c + 1 + i) % n_col), hid_col.at[i, pos], first)

    def hid_cross(pos, i):
        col = (c + 1 + i) % n_col
        return hid_copy(row_of(pos), col, partner, hid_partner.at[i, pos])

    def res_copy(i):
        j = (c + 1 + i) % n_col
        return pltpu.make_async_remote_copy(
            src_ref=residual.at[:, pl.ds(pl.multiple_of(j * width, width), width)],
            dst_ref=res.at[pl.ds(pl.multiple_of(c * res_rows, res_rows), res_rows), :],
            send_sem=col_send.at[0, i],
            recv_sem=col_recv.at[0, c],
            device_id=(r, j),
            device_id_type=MESH,
        )

    has_up, has_down = p < chips - 1, p > 0

    def each_way(guard_up, guard_down, fn):
        @pl.when(guard_up)
        def _():
            fn(0)

        @pl.when(guard_down)
        def _():
            fn(1)

    each_way(has_up, has_down, lambda way: hid_way(p, way, True).start())
    for k in range(CHUNKS):
        each_way(has_up, has_down, lambda way: ctx_copy(p, k, way, True).start())
        ctx_copy(p, k, 2, True).start()
    for i in range(n_col - 1):
        hid_side(p, i, True).start()
        res_copy(i).start()
    hid_way(p, 2, True).start()

    def arrive_hid(pos, way, onward):
        hid_way(pos, way).wait_recv()

        @pl.when(onward)
        def _():
            hid_way(pos, way).start()

        hid_way(pos, 2).start()
        for i in range(n_col - 1):
            hid_side(pos, i).start()

    def arrive_ctx(pos, k, way, onward):
        ctx_copy(pos, k, way).wait_recv()

        @pl.when(onward)
        def _():
            ctx_copy(pos, k, way).start()

        ctx_copy(pos, k, 2).start()

    def both(distance, fn):
        @pl.when(p >= distance)
        def _():
            fn(p - distance, 0, has_up)

        @pl.when(p + distance < chips)
        def _():
            fn(p + distance, 1, has_down)

    for distance in range(1, chips):
        both(distance, arrive_hid)
        if distance < chips - 1:
            for k in range(CHUNKS):
                both(distance, lambda pos, way, on: arrive_ctx(pos, k, way, on))

    own[0].wait()
    partner_row = r + 1 - 2 * core

    def product(j, k):
        cols = pl.ds(pl.multiple_of(j * width, width), width)
        return jnp.dot(
            ctx[:, k * chunk:(k + 1) * chunk],
            w[k * chunk:(k + 1) * chunk, cols],
            preferred_element_type=jnp.float32,
        )

    def part_copy(i):
        j = (c + 1 + i) % n_col
        return pltpu.make_async_remote_copy(
            src_ref=part_out.at[i],
            dst_ref=part_in.at[c],
            send_sem=col_send.at[1, i],
            recv_sem=col_recv.at[1, c],
            device_id=(r, j),
            device_id_type=MESH,
        )

    for k in range(CHUNKS):
        if chips > 1:
            both(chips - 1, lambda pos, way, on: arrive_ctx(pos, k, way, on))
        for pos in range(chips):
            row = pos * 2 + 1 - core
            there = ctx.at[rows_of(row), pl.ds(k * chunk, chunk)]
            pltpu.make_async_remote_copy(
                src_ref=there, dst_ref=there, send_sem=ctx_send.at[2, pos, k],
                recv_sem=ctx_recv.at[row, k], device_id=partner, device_id_type=MESH,
            ).wait_recv()
        w_copy(k).wait()
        if k < CHUNKS - 1:
            def step(j, _, k=k):
                if k == 0:
                    acc[j] = product(j, k)
                else:
                    acc[j] += product(j, k)
                return 0

            lax.fori_loop(0, n_col, step, 0)
        else:
            def last(i, _):
                j = (c + 1 + i) % n_col
                part_out[i] = (acc[j] + product(j, CHUNKS - 1)).astype(jnp.bfloat16)
                part_copy(i).start()
                return 0

            lax.fori_loop(0, n_col - 1, last, 0)
            acc[c] = acc[c] + product(c, CHUNKS - 1)

    for pos in range(chips):
        for i in range(n_col - 1):
            j = (c + 1 + i) % n_col
            hid_copy(row_of(pos), j, (r, j), hid_col.at[i, pos]).wait_recv()
            hid_cross(pos, i).start()
    for j in range(student_gain.shape[0]):
        sgain[:, j * LANES:(j + 1) * LANES] = student_gain[j:j + 1, :]
    gain_rows = width // LANES
    for j in range(gain_rows):
        tgain[:, j * LANES:(j + 1) * LANES] = teacher_gain[pl.ds(me * gain_rows + j, 1), :]
    for pos in range(chips):
        for j in range(n_col):
            hid_copy(pos * 2 + 1 - core, j, partner, hid_chain.at[2, pos]).wait_recv()
    own[1].wait()

    group = 8 // hid_rows if hid_rows < 8 else 1

    def widen(s, _):
        wide_rows = pl.ds(pl.multiple_of(s * group * hid_rows, 8), group * hid_rows)
        wide[wide_rows, :] = jnp.concatenate(
            [hid[s * group + i].astype(jnp.float32) for i in range(group)], axis=0
        )
        return 0

    lax.fori_loop(0, devices // group, widen, 0)

    tile = 16

    def normalize(t, _):
        rows = pl.ds(pl.multiple_of(t * tile, tile), tile)
        x = wide[rows, :]
        normed = x * lax.rsqrt(jnp.mean(x * x, axis=1, keepdims=True) + norm_eps)
        wide[rows, :] = normed
        student_out[rows, :] = (normed * sgain[...]).astype(jnp.bfloat16)
        return 0

    lax.fori_loop(0, tokens // tile, normalize, 0)
    proj_copy.wait()
    predicted[...] = jnp.dot(student_out[...], proj[...], preferred_element_type=jnp.float32)

    own[2].wait()
    for i in range(n_col - 1):
        j = (c + 1 + i) % n_col
        pltpu.make_async_remote_copy(
            src_ref=part_out.at[i], dst_ref=part_in.at[j], send_sem=col_send.at[1, i],
            recv_sem=col_recv.at[1, j], device_id=(r, j), device_id_type=MESH,
        ).wait_recv()
        rows = res.at[pl.ds(pl.multiple_of(j * res_rows, res_rows), res_rows), :]
        pltpu.make_async_remote_copy(
            src_ref=rows, dst_ref=rows, send_sem=col_send.at[0, i],
            recv_sem=col_recv.at[0, j], device_id=(r, j), device_id_type=MESH,
        ).wait_recv()
    summed = acc[c] + res[...].astype(jnp.float32)
    for i in range(n_col - 1):
        summed = summed + part_in[(c + 1 + i) % n_col].astype(jnp.float32)
    total[...] = summed
    squares = jnp.sum(summed * summed, axis=1, keepdims=True)
    for b in range(tokens // LANES):
        lanes = slice(b * LANES, (b + 1) * LANES)
        row = to_row(squares[lanes, :])
        sq_out[:, lanes] = row
        sq_in[me, :, lanes] = row

    def to_all(stage, src, dst):
        def copy(i):
            d = (me + 1 + i) % devices
            return pltpu.make_async_remote_copy(
                src_ref=src(d), dst_ref=dst.at[me],
                send_sem=all_send.at[stage], recv_sem=all_recv.at[stage],
                device_id=(d // n_col, d % n_col), device_id_type=MESH,
            )

        def send(i, _):
            copy(i).start()
            return 0

        lax.fori_loop(0, devices - 1, send, 0)

    def wait_all(sem, stage, dst):
        view = dst.at[pl.ds(0, devices - 1)]
        pltpu.make_async_copy(view, view, sem.at[stage]).wait()

    to_all(0, lambda d: sq_out, sq_in)
    wait_all(all_recv, 0, sq_in)
    sums = jnp.sum(sq_in[...], axis=0)
    factor = lax.rsqrt(sums / d_t + norm_eps)
    loss_part = jnp.zeros((1, 1), jnp.float32)
    for b in range(tokens // LANES):
        rows = slice(b * LANES, (b + 1) * LANES)
        target = (total[rows, :] * to_column(factor[:, rows]) * tgain[...]).astype(jnp.bfloat16)
        difference = predicted[rows, :] - target.astype(jnp.float32)
        loss_part = loss_part + jnp.sum(difference * difference, keepdims=True)
        error_out[rows, :] = (difference * (1.0 / 64.0)).astype(jnp.bfloat16)

    block = 512

    def gain_step(n, _):
        rows = pl.ds(pl.multiple_of(n * block, block), block)
        grad_normed = lax.dot_general(
            error_out[...], proj[rows, :], (((1,), (1,)), ((), ())),
            preferred_element_type=jnp.float32,
        )
        part = jnp.sum(grad_normed * wide[:, rows], axis=0, keepdims=True)
        for q in range(block // LANES):
            gp[n * (block // LANES) + q, 0:1, :] = part[:, q * LANES:(q + 1) * LANES]
            gp[n * (block // LANES) + q, 1:2, :] = jnp.broadcast_to(loss_part, (1, LANES))
        return 0

    lax.fori_loop(0, d_s // block, gain_step, 0)
    gp_in[me] = gp[me // repeat]
    to_all(1, lambda d: gp.at[d // repeat], gp_in)
    wait_all(all_recv, 1, gp_in)
    both_sums = jnp.sum(gp_in[...], axis=0)
    gg_out[...] = both_sums[0:1, :]
    gg[me] = both_sums[0:1, :]
    to_all(2, lambda d: gg_out, gg)
    loss_out[...] = both_sums[1:2, :] / (tokens * d_t)
    wait_all(all_recv, 2, gg)
    for j in range(segments):
        gain_out[j:j + 1, :] = gg[j * repeat]

    each_way(has_up, has_down, lambda way: hid_way(p, way).wait_send())
    hid_way(p, 2).wait_send()
    for k in range(CHUNKS):
        each_way(has_up, has_down, lambda way: ctx_copy(p, k, way).wait_send())
        ctx_copy(p, k, 2).wait_send()
    for i in range(n_col - 1):
        hid_side(p, i).wait_send()
        res_copy(i).wait_send()
        part_copy(i).wait_send()

    def left(pos, way, onward):
        @pl.when(onward)
        def _():
            hid_way(pos, way).wait_send()
            for k in range(CHUNKS):
                ctx_copy(pos, k, way).wait_send()

        hid_way(pos, 2).wait_send()
        for k in range(CHUNKS):
            ctx_copy(pos, k, 2).wait_send()
        for i in range(n_col - 1):
            hid_side(pos, i).wait_send()

    for distance in range(1, chips):
        both(distance, left)
    for pos in range(chips):
        for i in range(n_col - 1):
            hid_cross(pos, i).wait_send()
    wait_all(all_send, 0, sq_in)
    wait_all(all_send, 1, gp_in)
    wait_all(all_send, 2, gg)


def per_device(
    n_row, n_col,
    context, out_weight, residual, teacher_gain, student_hidden, student_gain, projector,
):
    devices = n_row * n_col
    chips = n_row // 2
    tokens = context.shape[0] * n_row
    d_s, width = projector.shape
    segments = min(devices, d_s // LANES)
    f32, bf16 = jnp.float32, jnp.bfloat16
    anywhere = pl.BlockSpec(memory_space=pl.ANY)
    vmem = pl.BlockSpec(memory_space=pltpu.VMEM)
    dma = pltpu.SemaphoreType.DMA
    student_all, error_term, grad_gain, loss = pl.pallas_call(
        functools.partial(body, n_row, n_col),
        out_shape=(
            jax.ShapeDtypeStruct((tokens, d_s), bf16),
            jax.ShapeDtypeStruct((tokens, width), bf16),
            jax.ShapeDtypeStruct((segments, LANES), f32),
            jax.ShapeDtypeStruct((1, LANES), f32),
        ),
        in_specs=[anywhere, anywhere, anywhere, vmem, anywhere, vmem, anywhere],
        out_specs=(vmem, vmem, vmem, vmem),
        scratch_shapes=[
            pltpu.VMEM((tokens, context.shape[1]), bf16),
            pltpu.VMEM(out_weight.shape, bf16),
            pltpu.VMEM((d_s, width), bf16),
            pltpu.VMEM((n_col, tokens, width), f32),
            pltpu.VMEM((n_col - 1, tokens, width), bf16),
            pltpu.VMEM((n_col, tokens, width), bf16),
            pltpu.VMEM((tokens, width), bf16),
            pltpu.VMEM((devices,) + student_hidden.shape, bf16),
            pltpu.VMEM((tokens, d_s), f32),
            pltpu.VMEM((8, LANES), f32),
            pltpu.VMEM((1, d_s), f32),
            pltpu.VMEM((1, width), f32),
            pltpu.VMEM((tokens, width), f32),
            pltpu.VMEM((tokens, width), f32),
            pltpu.VMEM((1, tokens), f32),
            pltpu.VMEM((devices, 1, tokens), f32),
            pltpu.VMEM((d_s // LANES, 2, LANES), f32),
            pltpu.VMEM((devices, 2, LANES), f32),
            pltpu.VMEM((1, LANES), f32),
            pltpu.VMEM((devices, 1, LANES), f32),
            dma((4,)),
            dma((CHUNKS,)),
            dma((3, chips, CHUNKS)),
            dma((n_row, CHUNKS)),
            dma((3, chips)),
            dma((n_col, chips)),
            dma((n_col, chips)),
            dma((devices,)),
            dma((2, n_col)),
            dma((2, n_col)),
            dma((3,)),
            dma((3,)),
        ],
        compiler_params=pltpu.CompilerParams(
            collective_id=0, has_side_effects=True, vmem_limit_bytes=48 * 1024 * 1024
        ),
    )(
        context, out_weight, residual, teacher_gain.reshape(-1, LANES), student_hidden,
        student_gain.reshape(-1, LANES), projector,
    )
    grad_proj = lax.dot_general(
        student_all, error_term, (((0,), (0,)), ((), ())), preferred_element_type=f32
    )
    return (grad_proj, grad_gain.reshape(-1), loss[0, 0])


def solution(mesh):
    placed = (
        P("row", "col"),
        P("col", "row"),
        P("col", "row"),
        P(),
        P(("row", "col"), None),
        P(),
        P(None, ("row", "col")),
    )
    return jax.shard_map(
        functools.partial(per_device, mesh.shape["row"], mesh.shape["col"]),
        mesh=mesh,
        in_specs=placed,
        out_specs=(P(None, ("row", "col")), P(), P()),
        check_vma=False,
    )
```

time: 206 us -> 66 us (0.32)
  waiting for transfers between devices: 108 us -> 0 us
  blocking collectives: 53.4 us -> 0 us
  Pallas kernels: 0 us -> 52.3 us
  matrix products: 19.4 us -> 4.67 us
  between operations: 15.6 us -> 1.82 us
  local copies, waits for them, and re-layouts: 1.98 us -> 6.91 us
  starting transfers between devices: 3.44 us -> 0 us
  other arithmetic: 2.4 us -> 0 us
    all_gather x2 -> x0, waiting for transfers between devices: 72.7 us -> none  [the longest x1 46.8 us: per_device(): lax.all_gather(student_hidden, ('row', 'col'), axis=0, tiled=True)]
    psum x2 -> x0, blocking collectives: 53.4 us -> none  [the longest x1 37.2 us: per_device(): grad_gain = lax.psum(gain_part, ('row', 'col'))]
    pallas_call x0 -> x1, Pallas kernels: none -> 52.3 us  [per_device(): pl.pallas_call(functools.partial(body, n_row, n_col), out_shape=(jax.Shap...]
    reduce_scatter x1 -> x0, waiting for transfers between devices: 28.9 us -> none  [per_device(): lax.psum_scatter(jnp.dot(context_all, out_weight, preferred_element_type=...]
    dot_general x3 -> x0, matrix products: 14.6 us -> none  [the longest x1 9.41 us: per_device(): jnp.dot(context_all, out_weight, preferred_element_type=jnp.float32)]
    unnamed x6 -> x13, local copies, waits for them, and re-layouts: 0.02 us -> 6.91 us
    all_to_all x1 -> x0, waiting for transfers between devices: 4.97 us -> none  [per_device(): lax.all_to_all(final_rows, 'col', split_axis=1, concat_axis=0, tiled=True)]
    all_to_all x1 -> x0, starting transfers between devices: 3.33 us -> none  [per_device(): lax.all_to_all(final_rows, 'col', split_axis=1, concat_axis=0, tiled=True)]
  transfers between devices with their start and end apart: 4 -> 0, of which waited for: 4 -> 0; matrix products, arithmetic and copies ran while one was open for 5% -> 0% of each run, Pallas kernels for 0% -> 0%
where the time goes in v1:
time: 66 us; the launch traced here: 65.7 us
  Pallas kernels  52.3 us (79%)
  local copies, waits for them, and re-layouts  6.91 us (10%)
  matrix products  4.67 us (7%)
  between operations  1.82 us (3%)
    pallas_call x1, Pallas kernels, per_device(): pl.pallas_call(functools.partial(body, n_row, n_col), out_shape=(jax.Shap...  52.3 us
    unnamed x13, local copies, waits for them, and re-layouts  6.91 us
    dot_general x1, matrix products, per_device(): lax.dot_general(student_all, error_term, (((0,), (0,)), ((), ())), prefer...  4.67 us

profile of v1, /device:TPU:0, one launch (start us, length us, event | category | flops | bytes accessed | tf_op | source)
XLA Modules:
  0.0 65.7 jit_solution(10152586502984385160)
XLA Ops:
  0.6 0.0 copy-start
  0.6 2.2 %copy-done = bf16[4096,512]{1,0:T(8,128)(2,1)S(1)} copy-done((bf16[4096,512]{1,0:T(8,128)(2,1)S(1)}, bf16[4096,512]{1,0:T(8,128)(2,1)}, u32[]{:S(2)}) %copy-start) | copy-done | bytes 4194328
  2.8 0.0 copy-start.1
  2.8 0.9 %copy-done.1 = bf16[16,4096]{1,0:T(8,128)(2,1)S(1)} copy-done((bf16[16,4096]{1,0:T(8,128)(2,1)S(1)}, bf16[16,4096]{1,0:T(8,128)(2,1)}, u32[]{:S(2)}) %copy-start.1) | copy-done | bytes 131096
  3.7 0.0 copy-start.2
  3.7 0.9 %copy-done.2 = bf16[32,2048]{1,0:T(8,128)(2,1)S(1)} copy-done((bf16[32,2048]{1,0:T(8,128)(2,1)S(1)}, bf16[32,2048]{1,0:T(8,128)(2,1)}, u32[]{:S(2)}) %copy-start.2) | copy-done | bytes 131096
  4.6 0.0 copy-start.3
  4.6 0.8 %copy-done.3 = f32[16384]{0:T(1024)S(1)} copy-done((f32[16384]{0:T(1024)S(1)}, f32[16384]{0:T(1024)}, u32[]{:S(2)}) %copy-start.3) | copy-done | bytes 65560
  5.5 0.0 copy-start.4
  5.5 0.8 %copy-done.4 = bf16[4,4096]{1,0:T(4,128)(2,1)S(1)} copy-done((bf16[4,4096]{1,0:T(4,128)(2,1)S(1)}, bf16[4,4096]{1,0:T(4,128)(2,1)}, u32[]{:S(2)}) %copy-start.4) | copy-done | bytes 32792
  6.2 0.0 copy-start.5
  6.2 0.7 %copy-done.5 = f32[4096]{0:T(1024)S(1)} copy-done((f32[4096]{0:T(1024)S(1)}, f32[4096]{0:T(1024)}, u32[]{:S(2)}) %copy-start.5) | copy-done | bytes 16408
  6.9 52.3 %shard_map.94 = (bf16[128,4096]{1,0:T(8,128)(2,1)S(1)}, bf16[128,512]{1,0:T(8,128)(2,1)S(1)}, f32[32,128]{1,0:T(8,128)S(1)}, f32[1,128]{1,0:T(1,128)S(1)}) custom-call(bf16[16,4096]{1,0:T(8,128)(2,1)S(1)} %copy-done.1, bf16[4096,2048]{1,0:T(8,128)(2,1)} %weight.1, bf16[32,2048]{1,0:T(8,128)(2,1)S(1)} %copy-done.2, f32[128,128]{1,0:T(8,128)S(1)} %bitcast.7, ...), custom_call_target="tpu_custom_call" | custom-call | tf_op jit(solution)/shard_map/pallas_call | solution.py:411
  59.2 4.7 %fusion = f32[4096,512]{1,0:T(8,128)} fusion(bf16[128,4096]{1,0:T(8,128)(2,1)S(1)} %get-tuple-element.7, bf16[128,512]{1,0:T(8,128)(2,1)S(1)} %get-tuple-element.8), kind=kOutput, calls=%fused_computation | convolution fusion | flops 536870912 | bytes 9568256 | tf_op jit(solution)/shard_map/dot_general | solution.py:462
  63.9 0.6 copy.12
Async XLA Ops:
  0.6 2.2 %copy-start = (bf16[4096,512]{1,0:T(8,128)(2,1)S(1)}, bf16[4096,512]{1,0:T(8,128)(2,1)}, u32[]{:S(2)}) copy-start(bf16[4096,512]{1,0:T(8,128)(2,1)} %projector.1) | copy-start | bytes 12582916
  2.8 0.9 %copy-start.1 = (bf16[16,4096]{1,0:T(8,128)(2,1)S(1)}, bf16[16,4096]{1,0:T(8,128)(2,1)}, u32[]{:S(2)}) copy-start(bf16[16,4096]{1,0:T(8,128)(2,1)} %context.1) | copy-start | bytes 393220
  3.7 0.9 %copy-start.2 = (bf16[32,2048]{1,0:T(8,128)(2,1)S(1)}, bf16[32,2048]{1,0:T(8,128)(2,1)}, u32[]{:S(2)}) copy-start(bf16[32,2048]{1,0:T(8,128)(2,1)} %residual.1) | copy-start | bytes 393220
  4.6 0.8 %copy-start.3 = (f32[16384]{0:T(1024)S(1)}, f32[16384]{0:T(1024)}, u32[]{:S(2)}) copy-start(f32[16384]{0:T(1024)} %param.10) | copy-start | bytes 196612
  5.5 0.8 %copy-start.4 = (bf16[4,4096]{1,0:T(4,128)(2,1)S(1)}, bf16[4,4096]{1,0:T(4,128)(2,1)}, u32[]{:S(2)}) copy-start(bf16[4,4096]{1,0:T(4,128)(2,1)} %hidden.1) | copy-start | bytes 98308
  6.2 0.7 %copy-start.5 = (f32[4096]{0:T(1024)S(1)}, f32[4096]{0:T(1024)}, u32[]{:S(2)}) copy-start(f32[4096]{0:T(1024)} %param.12) | copy-start | bytes 49156

commit v2 on v1

--- a/solution.py
+++ b/solution.py
@@ -10,6 +10,8 @@
 norm_eps = 1e-05
 LANES = 128
 CHUNKS = 4
+HIDDEN_AT = 2
+AHEAD = 3
 MESH = pl.DeviceIdType.MESH
 
 
@@ -25,7 +27,7 @@
     n_row, n_col,
     context, weight, residual, teacher_gain, hidden, student_gain, projector,
     student_out, error_out, gain_out, loss_out,
-    ctx, w, proj, acc, part_out, part_in, res, hid, wide, inverse, sgain, tgain,
+    student, error, ctx, w, proj, acc, part_out, part_in, res, hid, wide, sgain, tgain,
     predicted, total, sq_out, sq_in, gp, gp_in, gg_out, gg,
     local_sem, w_sem, ctx_send, ctx_recv, hid_chain, hid_partner, hid_col, hid_recv,
     col_send, col_recv, all_send, all_recv,
@@ -76,16 +78,6 @@
 
     barrier = pltpu.get_barrier_semaphore()
 
-    def greet(i, _):
-        d = (me + 1 + i) % devices
-        pl.semaphore_signal(
-            barrier, inc=1, device_id=(d // n_col, d % n_col), device_id_type=MESH
-        )
-        return 0
-
-    lax.fori_loop(0, devices - 1, greet, 0)
-    pl.semaphore_wait(barrier, devices - 1)
-
     up, down, partner = (r + 2, c), (r - 2, c), (r + 1 - 2 * core, c)
     targets = {0: up, 1: down, 2: partner}
 
@@ -136,6 +128,23 @@
 
     has_up, has_down = p < chips - 1, p > 0
 
+    def greet(device):
+        pl.semaphore_signal(barrier, inc=1, device_id=device, device_id_type=MESH)
+
+    @pl.when(has_up)
+    def _():
+        greet(up)
+
+    @pl.when(has_down)
+    def _():
+        greet(down)
+
+    greet(partner)
+    for i in range(n_col - 1):
+        greet((r, (c + 1 + i) % n_col))
+    peers = n_col + has_up.astype(jnp.int32) + has_down.astype(jnp.int32)
+    pl.semaphore_wait(barrier, peers)
+
     def each_way(guard_up, guard_down, fn):
         @pl.when(guard_up)
         def _():
@@ -145,10 +154,12 @@
         def _():
             fn(1)
 
-    each_way(has_up, has_down, lambda way: hid_way(p, way, True).start())
-    for k in range(CHUNKS):
+    def own_chunk(k):
         each_way(has_up, has_down, lambda way: ctx_copy(p, k, way, True).start())
         ctx_copy(p, k, 2, True).start()
+
+    for k in range(AHEAD):
+        own_chunk(k)
     for i in range(n_col - 1):
         hid_side(p, i, True).start()
         res_copy(i).start()
@@ -183,14 +194,7 @@
         def _():
             fn(p + distance, 1, has_down)
 
-    for distance in range(1, chips):
-        both(distance, arrive_hid)
-        if distance < chips - 1:
-            for k in range(CHUNKS):
-                both(distance, lambda pos, way, on: arrive_ctx(pos, k, way, on))
-
     own[0].wait()
-    partner_row = r + 1 - 2 * core
 
     def product(j, k):
         cols = pl.ds(pl.multiple_of(j * width, width), width)
@@ -211,9 +215,7 @@
             device_id_type=MESH,
         )
 
-    for k in range(CHUNKS):
-        if chips > 1:
-            both(chips - 1, lambda pos, way, on: arrive_ctx(pos, k, way, on))
+    def multiply(k):
         for pos in range(chips):
             row = pos * 2 + 1 - core
             there = ctx.at[rows_of(row), pl.ds(k * chunk, chunk)]
@@ -241,6 +243,21 @@
             lax.fori_loop(0, n_col - 1, last, 0)
             acc[c] = acc[c] + product(c, CHUNKS - 1)
 
+    for wave in range(1, CHUNKS + chips - 1):
+        if wave >= chips:
+            multiply(wave - chips)
+        for distance in range(1, chips):
+            k = wave - distance
+            if 0 <= k < CHUNKS:
+                both(distance, lambda pos, way, on: arrive_ctx(pos, k, way, on))
+            if k == HIDDEN_AT:
+                both(distance, arrive_hid)
+        if AHEAD - 1 + wave < CHUNKS:
+            own_chunk(AHEAD - 1 + wave)
+        if wave == max(HIDDEN_AT, 1):
+            each_way(has_up, has_down, lambda way: hid_way(p, way, True).start())
+    multiply(CHUNKS - 1)
+
     for pos in range(chips):
         for i in range(n_col - 1):
             j = (c + 1 + i) % n_col
@@ -274,12 +291,14 @@
         x = wide[rows, :]
         normed = x * lax.rsqrt(jnp.mean(x * x, axis=1, keepdims=True) + norm_eps)
         wide[rows, :] = normed
-        student_out[rows, :] = (normed * sgain[...]).astype(jnp.bfloat16)
+        student[rows, :] = (normed * sgain[...]).astype(jnp.bfloat16)
         return 0
 
     lax.fori_loop(0, tokens // tile, normalize, 0)
+    student_copy = pltpu.make_async_copy(student, student_out, local_sem.at[4])
+    student_copy.start()
     proj_copy.wait()
-    predicted[...] = jnp.dot(student_out[...], proj[...], preferred_element_type=jnp.float32)
+    predicted[...] = jnp.dot(student[...], proj[...], preferred_element_type=jnp.float32)
 
     own[2].wait()
     for i in range(n_col - 1):
@@ -333,14 +352,17 @@
         target = (total[rows, :] * to_column(factor[:, rows]) * tgain[...]).astype(jnp.bfloat16)
         difference = predicted[rows, :] - target.astype(jnp.float32)
         loss_part = loss_part + jnp.sum(difference * difference, keepdims=True)
-        error_out[rows, :] = (difference * (1.0 / 64.0)).astype(jnp.bfloat16)
+        error[rows, :] = (difference * (1.0 / 64.0)).astype(jnp.bfloat16)
+
+    error_copy = pltpu.make_async_copy(error, error_out, local_sem.at[5])
+    error_copy.start()
 
     block = 512
 
     def gain_step(n, _):
         rows = pl.ds(pl.multiple_of(n * block, block), block)
         grad_normed = lax.dot_general(
-            error_out[...], proj[rows, :], (((1,), (1,)), ((), ())),
+            error[...], proj[rows, :], (((1,), (1,)), ((), ())),
             preferred_element_type=jnp.float32,
         )
         part = jnp.sum(grad_normed * wide[:, rows], axis=0, keepdims=True)
@@ -362,6 +384,8 @@
     for j in range(segments):
         gain_out[j:j + 1, :] = gg[j * repeat]
 
+    student_copy.wait()
+    error_copy.wait()
     each_way(has_up, has_down, lambda way: hid_way(p, way).wait_send())
     hid_way(p, 2).wait_send()
     for k in range(CHUNKS):
@@ -417,8 +441,10 @@
             jax.ShapeDtypeStruct((1, LANES), f32),
         ),
         in_specs=[anywhere, anywhere, anywhere, vmem, anywhere, vmem, anywhere],
-        out_specs=(vmem, vmem, vmem, vmem),
+        out_specs=(anywhere, anywhere, vmem, vmem),
         scratch_shapes=[
+            pltpu.VMEM((tokens, d_s), bf16),
+            pltpu.VMEM((tokens, width), bf16),
             pltpu.VMEM((tokens, context.shape[1]), bf16),
             pltpu.VMEM(out_weight.shape, bf16),
             pltpu.VMEM((d_s, width), bf16),
@@ -428,7 +454,6 @@
             pltpu.VMEM((tokens, width), bf16),
             pltpu.VMEM((devices,) + student_hidden.shape, bf16),
             pltpu.VMEM((tokens, d_s), f32),
-            pltpu.VMEM((8, LANES), f32),
             pltpu.VMEM((1, d_s), f32),
             pltpu.VMEM((1, width), f32),
             pltpu.VMEM((tokens, width), f32),
@@ -439,7 +464,7 @@
             pltpu.VMEM((devices, 2, LANES), f32),
             pltpu.VMEM((1, LANES), f32),
             pltpu.VMEM((devices, 1, LANES), f32),
-            dma((4,)),
+            dma((6,)),
             dma((CHUNKS,)),
             dma((3, chips, CHUNKS)),
             dma((n_row, CHUNKS)),
@@ -453,7 +478,7 @@
             dma((3,)),
         ],
         compiler_params=pltpu.CompilerParams(
-            collective_id=0, has_side_effects=True, vmem_limit_bytes=48 * 1024 * 1024
+            collective_id=0, has_side_effects=True, vmem_limit_bytes=67_000_000
         ),
     )(
         context, out_weight, residual, teacher_gain.reshape(-1, LANES), student_hidden,

time: 66 us -> 60 us (0.909)
  local copies, waits for them, and re-layouts: 6.91 us -> 0.62 us
  matrix products: 4.67 us -> 5.9 us
  Pallas kernels: 52.3 us -> 51.5 us
    unnamed x13 -> x5, local copies, waits for them, and re-layouts: 6.91 us -> 0.62 us
    dot_general x1, matrix products: 4.67 us -> 5.9 us  [per_device(): lax.dot_general(student_all, error_term, (((0,), (0,)), ((), ())), prefer...]
    pallas_call x1, Pallas kernels: 52.3 us -> 51.5 us  [per_device(): pl.pallas_call(functools.partial(body, n_row, n_col), out_shape=(jax.Shap...]
where the time goes in v2:
time: 60 us; the launch traced here: 59.8 us
  Pallas kernels  51.5 us (86%)
  matrix products  5.9 us (10%)
  between operations  1.82 us (3%)
  local copies, waits for them, and re-layouts  0.62 us (1%)
    pallas_call x1, Pallas kernels, per_device(): pl.pallas_call(functools.partial(body, n_row, n_col), out_shape=(jax.Shap...  51.5 us
    dot_general x1, matrix products, per_device(): lax.dot_general(student_all, error_term, (((0,), (0,)), ((), ())), prefer...  5.9 us

profile of v2, /device:TPU:0, one launch (start us, length us, event | category | flops | bytes accessed | tf_op | source)
XLA Modules:
  0.0 59.8 jit_solution(15866018457025877835)
XLA Ops:
  0.6 51.5 %shard_map.94 = (bf16[128,4096]{1,0:T(8,128)(2,1)}, bf16[128,512]{1,0:T(8,128)(2,1)}, f32[32,128]{1,0:T(8,128)}, f32[1,128]{1,0:T(1,128)}) custom-call(bf16[16,4096]{1,0:T(8,128)(2,1)} %context.1, bf16[4096,2048]{1,0:T(8,128)(2,1)} %weight.1, bf16[32,2048]{1,0:T(8,128)(2,1)} %residual.1, f32[128,128]{1,0:T(8,128)} %bitcast.7, bf16[4,4096]{1,0:T(4,128)(2,1)} %hidden.1, ...), custom_call_target="tpu_custom_call" | custom-call | tf_op jit(solution)/shard_map/pallas_call | solution.py:435
  52.1 0.0 copy-start
  52.1 0.0 copy-start.1
  52.2 5.9 %fusion = f32[4096,512]{1,0:T(8,128)} fusion(bf16[128,4096]{1,0:T(8,128)(2,1)} %get-tuple-element.7, bf16[128,512]{1,0:T(8,128)(2,1)} %get-tuple-element.8), kind=kOutput, calls=%fused_computation | convolution fusion | flops 536870912 | bytes 9568256 | tf_op jit(solution)/shard_map/dot_general | solution.py:487
  58.0 0.0 copy-done
  58.0 0.6 %copy.12 = f32[4096]{0:T(1024)} copy(f32[4096]{0:T(1024)S(1)} %bitcast.9) | data formatting | bytes 32768
  58.7 0.0 copy-done.1
Async XLA Ops:
  52.1 5.9 %copy-start = (f32[32,128]{1,0:T(8,128)S(1)}, f32[32,128]{1,0:T(8,128)}, u32[]{:S(2)}) copy-start(f32[32,128]{1,0:T(8,128)} %get-tuple-element.9) | copy-start | bytes 49156
  52.1 6.5 %copy-start.1 = (f32[1,128]{1,0:T(1,128)S(1)}, f32[1,128]{1,0:T(1,128)}, u32[]{:S(2)}) copy-start(f32[1,128]{1,0:T(1,128)} %get-tuple-element.10) | copy-start | bytes 1540
